TPU v7x, 32 devices: a whole 2x2x4 slice. The times are simulated.
32 devices in a mesh: dp: 4 (over x, core), blk: 8 (over z, y).
Axes of the slice: x: 2, y: 2, z: 4, core: 2. Of those that a mesh axis runs over, the one named last changes fastest.
Arguments:
- hidden_in: bfloat16 [2048, 8, 1024], P('blk', 'dp'), may hold values from -6 to 6
- first_values: bfloat16 [2048, 8, 1024], P('blk', 'dp'), may hold values from -13 to 13
- doc_lengths: int32 [8, 8], P('dp'), may hold values from 1 to 1024, 2048 in all within a row
- w_query: bfloat16 [1024, 1024], replicated, may hold values from -0.25 to 0.25
- w_key: bfloat16 [1024, 1024], replicated, may hold values from -0.25 to 0.25
- w_value: bfloat16 [1024, 1024], replicated, may hold values from -0.1875 to 0.1875
- w_out: bfloat16 [1024, 1024], replicated, may hold values from -0.75 to 0.75
- w_gate: bfloat16 [1024, 2816], replicated, may hold values from -0.1875 to 0.1875
- w_up: bfloat16 [1024, 2816], replicated, may hold values from -0.1875 to 0.1875
- w_down: bfloat16 [2816, 1024], replicated, may hold values from -0.109375 to 0.109375
- attn_gain: float32 [1024], replicated, may hold values from 0.5 to 1.5
- ffn_gain: float32 [1024], replicated, may hold values from 0.5 to 1.5
- out_cotangent: bfloat16 [2048, 8, 1024], P('blk', 'dp'), may hold values from -6 to 6
Outputs:
- block_out: bfloat16 [2048, 8, 1024], P('blk', 'dp')
- grad_input: float32 [2048, 8, 1024], P('blk', 'dp')
- grad_first: float32 [2048, 8, 1024], P('blk', 'dp')
- grad_query: float32 [1024, 1024], P('dp', 'blk')
- grad_key: float32 [1024, 1024], P('dp', 'blk')
- grad_value: float32 [1024, 1024], P('dp', 'blk')
- grad_project: float32 [1024, 1024], P('dp', 'blk')
- grad_gate: float32 [1024, 2816], P('dp', 'blk')
- grad_up: float32 [1024, 2816], P('dp', 'blk')
- grad_down: float32 [2816, 1024], P('dp', 'blk')
- grad_attn_gain: float32 [1024], replicated
- grad_ffn_gain: float32 [1024], replicated
- first_msq: float32 [], replicated
- mixed_msq: float32 [], replicated
Inputs may be any that keep to these rules, and one draw needn't show every extreme that they name: `doc_lengths`: the 8 lengths of a row sum to 2048.
All inputs are finite; a program needn't handle non-finite values.
Results may differ from a plain program's by a relative error of at most 0.033.
Values may be sent and summed in bfloat16 or wider, within the bound.
A program may use at most 320 MiB of HBM per device.

v0:
```python
import jax
import jax.numpy as jnp
from jax import lax
from jax.sharding import PartitionSpec as P

HEADS = 16
HEAD_DIM = 64
epsilon = 1e-06


def documents(doc_lengths, row_length):
    doc_ends = jnp.cumsum(doc_lengths, axis=1)
    places = jnp.arange(row_length, dtype=jnp.int32)
    passed = (doc_ends[:, None, :] <= places[None, :, None]).astype(jnp.int32)
    segment = jnp.sum(passed, axis=2)
    doc_start = jnp.sum(passed * doc_lengths[:, None, :], axis=2)
    return (segment, places[None, :] - doc_start)


def project(acts, weight):
    flat = acts.reshape(-1, acts.shape[-1])
    result = jnp.dot(flat, weight, preferred_element_type=jnp.float32)
    return result.reshape(acts.shape[:-1] + (weight.shape[1],))


def project_back(grads_in, weight):
    flat = grads_in.reshape(-1, grads_in.shape[-1])
    result = lax.dot_general(
        flat, weight, (((1,), (1,)), ((), ())), preferred_element_type=jnp.float32
    )
    return result.reshape(grads_in.shape[:-1] + (weight.shape[0],))


def weight_grad(acts, grads_in):
    flat_acts = acts.reshape(-1, acts.shape[-1])
    flat_grads = grads_in.reshape(-1, grads_in.shape[-1])
    return lax.dot_general(
        flat_acts, flat_grads, (((0,), (0,)), ((), ())), preferred_element_type=jnp.float32
    )


def rms_parts(values):
    inverse_rms = lax.rsqrt(jnp.mean(values * values, axis=-1, keepdims=True) + epsilon)
    return (values * inverse_rms, inverse_rms)


def norm_back(d_normed, normed, inverse_rms):
    return inverse_rms * (d_normed - normed * jnp.mean(d_normed * normed, axis=-1, keepdims=True))


def rope_tables(positions):
    half_dim = HEAD_DIM // 2
    inverse_freq = jnp.power(10000.0, -jnp.arange(half_dim, dtype=jnp.float32) * 2.0 / HEAD_DIM)
    angles = jnp.transpose(positions).astype(jnp.float32)[:, :, None] * inverse_freq[None, None, :]
    return (jnp.cos(angles)[:, :, None, :], jnp.sin(angles)[:, :, None, :])


def rotate(values, cos_table, sin_table):
    half_dim = HEAD_DIM // 2
    shaped = values.reshape(values.shape[:-1] + (HEADS, HEAD_DIM))
    first_half = shaped[..., :half_dim]
    second_half = shaped[..., half_dim:]
    turned = jnp.concatenate(
        [
            first_half * cos_table - second_half * sin_table,
            second_half * cos_table + first_half * sin_table,
        ],
        axis=-1,
    )
    return turned.reshape(values.shape)


def body(
    hidden_in,
    first_values,
    doc_lengths,
    w_query,
    w_key,
    w_value,
    w_out,
    w_gate,
    w_up,
    w_down,
    attn_gain,
    ffn_gain,
    out_cotangent,
):
    local_len, seq_count, model_width = hidden_in.shape
    cycle_size = lax.axis_size("blk")
    row_length = local_len * cycle_size
    offset = lax.axis_index("blk") * local_len
    score_scale = HEAD_DIM ** (-0.5)
    segment_all, position_all = documents(doc_lengths, row_length)
    segment_own = lax.dynamic_slice_in_dim(segment_all, offset, local_len, 1)
    position_own = lax.dynamic_slice_in_dim(position_all, offset, local_len, 1)
    query_index = offset + jnp.arange(local_len, dtype=jnp.int32)
    cos_table, sin_table = rope_tables(position_own)
    resid_in = hidden_in.astype(jnp.float32)
    normed_one, inv_one = rms_parts(resid_in)
    normed_in = (normed_one * attn_gain).astype(jnp.bfloat16)
    queries = rotate(project(normed_in, w_query), cos_table, sin_table).astype(jnp.bfloat16)
    keys_rot = rotate(project(normed_in, w_key), cos_table, sin_table).astype(jnp.bfloat16)
    first_f = first_values.astype(jnp.float32)
    mixed = 0.5 * project(normed_in, w_value) + 0.5 * first_f
    mixed_low = mixed.astype(jnp.bfloat16)
    first_sq = jnp.sum(first_f * first_f)
    mixed_sq = jnp.sum(mixed * mixed)
    query_four = queries.reshape(local_len, seq_count, HEADS, HEAD_DIM)

    def allowed_pairs(start, n_keys):
        key_index = start + jnp.arange(n_keys, dtype=jnp.int32)
        segment_key = lax.dynamic_slice_in_dim(segment_all, start, n_keys, 1)
        allowed = (key_index[None, None, :] <= query_index[None, :, None]) & (
            segment_key[:, None, :] == segment_own[:, :, None]
        )
        return allowed[:, None]

    def piece_step(running, key_piece, value_piece, start):
        run_max, run_sum, run_acc = running
        n_keys = key_piece.shape[0]
        allowed = allowed_pairs(start, n_keys)
        key_four = key_piece.reshape(n_keys, seq_count, HEADS, HEAD_DIM)
        value_four = value_piece.reshape(n_keys, seq_count, HEADS, HEAD_DIM)
        scores = (
            jnp.einsum("qshd,kshd->shqk", query_four, key_four, preferred_element_type=jnp.float32)
            * score_scale
        )
        new_max = jnp.maximum(run_max, jnp.max(jnp.where(allowed, scores, -1e30), axis=-1))
        weights = jnp.where(allowed, jnp.exp(scores - new_max[..., None]), 0.0)
        factor = jnp.exp(run_max - new_max)
        run_sum = run_sum * factor + jnp.sum(weights, axis=-1)
        run_acc = run_acc * factor[..., None] + jnp.einsum(
            "shqk,kshd->shqd",
            weights.astype(jnp.bfloat16),
            value_four,
            preferred_element_type=jnp.float32,
        )
        return (new_max, run_sum, run_acc)

    start_state = (
        jnp.full((seq_count, HEADS, local_len), -1e30, jnp.float32),
        jnp.zeros((seq_count, HEADS, local_len), jnp.float32),
        jnp.zeros((seq_count, HEADS, local_len, HEAD_DIM), jnp.float32),
    )
    running = start_state
    key_piece = lax.all_gather(keys_rot, "blk", axis=0, tiled=True)
    value_piece = lax.all_gather(mixed_low, "blk", axis=0, tiled=True)
    n_keys = key_piece.shape[0]
    step_rows = min(512, n_keys)
    n_steps = n_keys // step_rows

    def inner_step(fold_state, block_item):
        return (piece_step(fold_state, block_item[0], block_item[1], block_item[2]), None)

    starts = jnp.arange(n_steps, dtype=jnp.int32) * step_rows
    running, unused = lax.scan(
        inner_step,
        running,
        (
            key_piece.reshape(n_steps, step_rows, seq_count, model_width),
            value_piece.reshape(n_steps, step_rows, seq_count, model_width),
            starts,
        ),
    )
    run_max, run_sum, run_acc = running
    attn_four = jnp.transpose(run_acc / run_sum[..., None], (2, 0, 1, 3))
    attn_f = attn_four.reshape(local_len, seq_count, model_width)
    log_total = run_max + jnp.log(run_sum)
    attn_low = attn_f.astype(jnp.bfloat16)
    resid_mid = resid_in + project(attn_low, w_out)
    normed_two, inv_two = rms_parts(resid_mid)
    normed_mid = (normed_two * ffn_gain).astype(jnp.bfloat16)
    gate_pre = project(normed_mid, w_gate)
    up_pre = project(normed_mid, w_up)
    gate_act = jax.nn.silu(gate_pre)
    inner_low = (gate_act * up_pre).astype(jnp.bfloat16)
    block_out = (resid_mid + project(inner_low, w_down)).astype(jnp.bfloat16)
    grad_down = weight_grad(inner_low, out_cotangent)
    d_inner = project_back(out_cotangent, w_down)
    sigmoid_gate = jax.nn.sigmoid(gate_pre)
    d_gate = (d_inner * up_pre * sigmoid_gate * (1.0 + gate_pre * (1.0 - sigmoid_gate))).astype(
        jnp.bfloat16
    )
    d_up = (d_inner * gate_act).astype(jnp.bfloat16)
    grad_gate = weight_grad(normed_mid, d_gate)
    grad_up = weight_grad(normed_mid, d_up)
    d_normed_mid = project_back(d_gate, w_gate) + project_back(d_up, w_up)
    gain_two_grad = jnp.sum((d_normed_mid * normed_two).reshape(-1, model_width), axis=0)
    d_resid_mid = out_cotangent.astype(jnp.float32) + norm_back(
        d_normed_mid * ffn_gain, normed_two, inv_two
    )
    d_branch = d_resid_mid.astype(jnp.bfloat16)
    grad_project = weight_grad(attn_low, d_branch)
    d_attn = project_back(d_branch, w_out).astype(jnp.bfloat16)
    d_attn_four = d_attn.reshape(local_len, seq_count, HEADS, HEAD_DIM)
    delta_rows = jnp.transpose(
        jnp.sum(d_attn_four.astype(jnp.float32) * attn_four, axis=-1), (1, 2, 0)
    )
    back_keys, back_values = (
        lax.all_gather(keys_rot, "blk", axis=0, tiled=True),
        lax.all_gather(mixed_low, "blk", axis=0, tiled=True),
    )
    block_rows = min(512, row_length)
    n_blocks = row_length // block_rows
    block_starts = jnp.arange(n_blocks, dtype=jnp.int32) * block_rows

    def block_scores(key_four, value_four, start):
        allowed = allowed_pairs(start, block_rows)
        scores = (
            jnp.einsum("qshd,kshd->shqk", query_four, key_four, preferred_element_type=jnp.float32)
            * score_scale
        )
        probs = jnp.where(allowed, jnp.exp(scores - log_total[..., None]), 0.0)
        d_probs = jnp.einsum(
            "qshd,kshd->shqk", d_attn_four, value_four, preferred_element_type=jnp.float32
        )
        d_scores = (probs * (d_probs - delta_rows[..., None])).astype(jnp.bfloat16)
        return (probs, d_scores)

    def back_step(d_query_acc, block_item):
        key_block, value_block, start = block_item
        key_four = key_block.reshape(block_rows, seq_count, HEADS, HEAD_DIM)
        value_four = value_block.reshape(block_rows, seq_count, HEADS, HEAD_DIM)
        probs, d_scores = block_scores(key_four, value_four, start)
        d_query_acc = (
            d_query_acc
            + jnp.einsum("shqk,kshd->qshd", d_scores, key_four, preferred_element_type=jnp.float32)
            * score_scale
        )
        d_keys = (
            jnp.einsum("shqk,qshd->kshd", d_scores, query_four, preferred_element_type=jnp.float32)
            * score_scale
        )
        d_vals = jnp.einsum(
            "shqk,qshd->kshd",
            probs.astype(jnp.bfloat16),
            d_attn_four,
            preferred_element_type=jnp.float32,
        )
        joined = jnp.concatenate(
            [
                d_keys.reshape(block_rows, seq_count, model_width),
                d_vals.reshape(block_rows, seq_count, model_width),
            ],
            axis=-1,
        )
        return (d_query_acc, joined)

    d_query_rot, terms = lax.scan(
        back_step,
        jnp.zeros((local_len, seq_count, HEADS, HEAD_DIM), jnp.float32),
        (
            back_keys.reshape(n_blocks, block_rows, seq_count, model_width),
            back_values.reshape(n_blocks, block_rows, seq_count, model_width),
            block_starts,
        ),
    )
    terms = terms.reshape(row_length, seq_count, 2 * model_width)
    kv_grad = lax.psum_scatter(
        terms.astype(jnp.bfloat16), "blk", scatter_dimension=0, tiled=True
    ).astype(jnp.float32)
    d_key_rot = kv_grad[..., :model_width]
    d_mixed = kv_grad[..., model_width:]
    d_query_low = rotate(
        d_query_rot.reshape(local_len, seq_count, model_width), cos_table, -sin_table
    ).astype(jnp.bfloat16)
    d_key_low = rotate(d_key_rot, cos_table, -sin_table).astype(jnp.bfloat16)
    d_value_low = (0.5 * d_mixed).astype(jnp.bfloat16)
    grad_first = 0.5 * d_mixed
    grad_query = weight_grad(normed_in, d_query_low)
    grad_key = weight_grad(normed_in, d_key_low)
    grad_value = weight_grad(normed_in, d_value_low)
    d_normed_in = (
        project_back(d_query_low, w_query)
        + project_back(d_key_low, w_key)
        + project_back(d_value_low, w_value)
    )
    gain_one_grad = jnp.sum((d_normed_in * normed_one).reshape(-1, model_width), axis=0)
    grad_input = d_resid_mid + norm_back(d_normed_in * attn_gain, normed_one, inv_one)
    weight_grads = (grad_query, grad_key, grad_value, grad_project, grad_gate, grad_up, grad_down)
    partial_grads = (
        lax.psum_scatter(
            weight_grads[0].astype(jnp.bfloat16), "dp", scatter_dimension=0, tiled=True
        ).astype(jnp.float32),
        lax.psum_scatter(
            weight_grads[1].astype(jnp.bfloat16), "dp", scatter_dimension=0, tiled=True
        ).astype(jnp.float32),
        lax.psum_scatter(
            weight_grads[2].astype(jnp.bfloat16), "dp", scatter_dimension=0, tiled=True
        ).astype(jnp.float32),
        lax.psum_scatter(
            weight_grads[3].astype(jnp.bfloat16), "dp", scatter_dimension=0, tiled=True
        ).astype(jnp.float32),
        lax.psum_scatter(
            weight_grads[4].astype(jnp.bfloat16), "dp", scatter_dimension=0, tiled=True
        ).astype(jnp.float32),
        lax.psum_scatter(
            weight_grads[5].astype(jnp.bfloat16), "dp", scatter_dimension=0, tiled=True
        ).astype(jnp.float32),
        lax.psum_scatter(
            weight_grads[6].astype(jnp.bfloat16), "dp", scatter_dimension=0, tiled=True
        ).astype(jnp.float32),
    )
    summed = (
        lax.psum_scatter(
            partial_grads[0].astype(jnp.bfloat16), "blk", scatter_dimension=1, tiled=True
        ).astype(jnp.float32),
        lax.psum_scatter(
            partial_grads[1].astype(jnp.bfloat16), "blk", scatter_dimension=1, tiled=True
        ).astype(jnp.float32),
        lax.psum_scatter(
            partial_grads[2].astype(jnp.bfloat16), "blk", scatter_dimension=1, tiled=True
        ).astype(jnp.float32),
        lax.psum_scatter(
            partial_grads[3].astype(jnp.bfloat16), "blk", scatter_dimension=1, tiled=True
        ).astype(jnp.float32),
        lax.psum_scatter(
            partial_grads[4].astype(jnp.bfloat16), "blk", scatter_dimension=1, tiled=True
        ).astype(jnp.float32),
        lax.psum_scatter(
            partial_grads[5].astype(jnp.bfloat16), "blk", scatter_dimension=1, tiled=True
        ).astype(jnp.float32),
        lax.psum_scatter(
            partial_grads[6].astype(jnp.bfloat16), "blk", scatter_dimension=1, tiled=True
        ).astype(jnp.float32),
    )
    totals = lax.psum((gain_one_grad, gain_two_grad, first_sq, mixed_sq), ("dp", "blk"))
    n_entries = row_length * seq_count * lax.axis_size("dp") * model_width
    return (
        block_out,
        grad_input,
        grad_first,
        summed[0],
        summed[1],
        summed[2],
        summed[3],
        summed[4],
        summed[5],
        summed[6],
        totals[0],
        totals[1],
        totals[2] / n_entries,
        totals[3] / n_entries,
    )


def solution(mesh):
    in_specs = (
        P("blk", "dp", None),
        P("blk", "dp", None),
        P("dp", None),
        P(),
        P(),
        P(),
        P(),
        P(),
        P(),
        P(),
        P(),
        P(),
        P("blk", "dp", None),
    )
    out_specs = (
        P("blk", "dp", None),
        P("blk", "dp", None),
        P("blk", "dp", None),
        P("dp", "blk"),
        P("dp", "blk"),
        P("dp", "blk"),
        P("dp", "blk"),
        P("dp", "blk"),
        P("dp", "blk"),
        P("dp", "blk"),
        P(),
        P(),
        P(),
        P(),
    )
    return jax.shard_map(body, mesh=mesh, in_specs=in_specs, out_specs=out_specs, check_vma=False)
```

profile of v0, /device:TPU:0, one launch (start us, length us, event | category | flops | bytes accessed | tf_op | source)
XLA Modules:
  0.0 1740.5 jit_solution(13050748668814698923)
XLA Ops:
  42.2 99.5 %all-gather.5.cloned.1.call-done = bf16[2048,2,1024]{2,0,1:T(8,128)(2,1)} async-done(((bf16[256,2,1024]{2,0,1:T(8,128)(2,1)}), bf16[2048,2,1024]{2,0,1:T(8,128)(2,1)}) %all-gather.5.cloned.1.call-update) | async-done | bytes 8388624 | tf_op jit(solution)/shard_map/all_gather | solution.py:147
  141.7 11.7 copy.140
  153.4 114.2 %all-gather.3.cloned.1.call-done = bf16[2048,2,1024]{2,0,1:T(8,128)(2,1)} async-done(((bf16[256,2,1024]{2,0,1:T(8,128)(2,1)}), bf16[2048,2,1024]{2,0,1:T(8,128)(2,1)}) %all-gather.3.cloned.1.call-update) | async-done | bytes 8388624 | tf_op jit(solution)/shard_map/all_gather | solution.py:146
  279.1 144.7 %while.28 = (s32[]{:T(128)}, f32[2,16,256]{2,1,0:T(8,128)S(1)}, f32[2,16,256]{2,1,0:T(8,128)S(1)}, f32[2,16,256,64]{2,3,1,0:T(8,128)}, s32[4]{0:T(128)S(1)}, /*i...) while((s32[]{:T(128)}, f32[2,16,256]{2,1,0:T(8,128)S(1)}, ...), condition=%wide.region_7.8_spmd.clone, body=%wide.region_4.0_spmd.clone.sunk | while | flops 1122149120 | bytes 70013144 | solution.py:156
  339.4 11.7 fusion.161
  375.7 11.7 fusion.161
  412.0 11.7 fusion.161
  465.8 192.9 %while.29 = (s32[]{:T(128)}, f32[256,2,16,64]{0,3,2,1:T(8,128)}, bf16[4,512,2,2048]{1,3,2,0:T(8,128)(2,1)}, bf16[4,512,2,1024]{1,3,2,0:T(8,128)(2,1)}, s32[4]{0:...) while((s32[]{:T(128)}, f32[256,2,16,64]{0,3,2,1:T(8,128)}, ...), condition=%wide.region_12.13_spmd.clone, body=%wide.region_11.12_spmd.clone.sunk | while | flops 2739012352 | bytes 129093912 | solution.py:249
  658.7 21.6 %copy.148 = bf16[4,512,2,2048]{3,1,0,2:T(8,128)(2,1)} copy(bf16[4,512,2,2048]{1,3,2,0:T(8,128)(2,1)} %get-tuple-element.145) | data formatting | bytes 33554432 | tf_op jit(solution)/shard_map/convert_element_type | solution.py:260
  709.0 251.6 %reduce-scatter.30.cloned.1.call-done = bf16[256,2,2048]{2,0,1:T(8,128)(2,1)} async-done(((bf16[2048,2,2048]{2,0,1:T(8,128)(2,1)}), bf16[256,2,2048]{2,0,1:T(8,128)(2,1)}) %reduce-scatter.30.cloned.1.call-update) | async-done | bytes 2097168 | tf_op jit(solution)/shard_map/reduce_scatter | solution.py:259
  967.9 26.4 %reduce-scatter.38.cloned.1.call-done = bf16[256,1024]{1,0:T(8,128)(2,1)} async-done(((bf16[1024,1024]{1,0:T(8,128)(2,1)}), bf16[256,1024]{1,0:T(8,128)(2,1)}) %reduce-scatter.38.cloned.1.call-update) | async-done | bytes 524304 | tf_op jit(solution)/shard_map/reduce_scatter | solution.py:291
  996.4 55.2 %reduce-scatter.40.cloned.1.call-done = bf16[256,2816]{1,0:T(8,128)(2,1)} async-done(((bf16[1024,2816]{1,0:T(8,128)(2,1)}), bf16[256,2816]{1,0:T(8,128)(2,1)}) %reduce-scatter.40.cloned.1.call-update) | async-done | bytes 1441808 | tf_op jit(solution)/shard_map/reduce_scatter | solution.py:294
  1054.2 54.8 %reduce-scatter.42.cloned.1.call-done = bf16[256,2816]{1,0:T(8,128)(2,1)} async-done(((bf16[1024,2816]{1,0:T(8,128)(2,1)}), bf16[256,2816]{1,0:T(8,128)(2,1)}) %reduce-scatter.42.cloned.1.call-update) | async-done | bytes 1441808 | tf_op jit(solution)/shard_map/reduce_scatter | solution.py:297
  1111.7 54.8 %reduce-scatter.44.cloned.1.call-done = bf16[704,1024]{1,0:T(8,128)(2,1)} async-done(((bf16[2816,1024]{1,0:T(8,128)(2,1)}), bf16[704,1024]{1,0:T(8,128)(2,1)}) %reduce-scatter.44.cloned.1.call-update) | async-done | bytes 1441808 | tf_op jit(solution)/shard_map/reduce_scatter | solution.py:300
  1187.5 13.2 reduce-scatter.36.cloned.1.call-done
  1214.4 51.5 %reduce-scatter.52.cloned.1.call-done = bf16[128,256]{1,0:T(8,128)(2,1)} async-done(((bf16[1024,256]{1,0:T(8,128)(2,1)}), bf16[128,256]{1,0:T(8,128)(2,1)}) %reduce-scatter.52.cloned.1.call-update) | async-done | bytes 65552
  1267.6 66.0 %reduce-scatter.54.cloned.1.call-done = bf16[352,256]{1,0:T(8,128)(2,1)} async-done(((bf16[2816,256]{1,0:T(8,128)(2,1)}), bf16[352,256]{1,0:T(8,128)(2,1)}) %reduce-scatter.54.cloned.1.call-update) | async-done | bytes 180240
  1335.5 65.7 %reduce-scatter.56.cloned.1.call-done = bf16[352,256]{1,0:T(8,128)(2,1)} async-done(((bf16[2816,256]{1,0:T(8,128)(2,1)}), bf16[352,256]{1,0:T(8,128)(2,1)}) %reduce-scatter.56.cloned.1.call-update) | async-done | bytes 180240
  1403.2 65.4 %reduce-scatter.58.cloned.1.call-done = bf16[128,704]{1,0:T(8,128)(2,1)} async-done(((bf16[1024,704]{1,0:T(8,128)(2,1)}), bf16[128,704]{1,0:T(8,128)(2,1)}) %reduce-scatter.58.cloned.1.call-update) | async-done | bytes 180240
  1470.5 31.6 %reduce-scatter.34.cloned.1.call-done = bf16[256,1024]{1,0:T(8,128)(2,1)} async-done(((bf16[1024,1024]{1,0:T(8,128)(2,1)}), bf16[256,1024]{1,0:T(8,128)(2,1)}) %reduce-scatter.34.cloned.1.call-update) | async-done | bytes 524304 | tf_op jit(solution)/shard_map/reduce_scatter | solution.py:285
  1514.2 21.9 %reduce-scatter.32.cloned.1.call-done = bf16[256,1024]{1,0:T(8,128)(2,1)} async-done(((bf16[1024,1024]{1,0:T(8,128)(2,1)}), bf16[256,1024]{1,0:T(8,128)(2,1)}) %reduce-scatter.32.cloned.1.call-update) | async-done | bytes 524304 | tf_op jit(solution)/shard_map/reduce_scatter | solution.py:282
  1544.2 39.7 %all-reduce = (f32[1024]{0:T(1024)}, f32[1024]{0:T(1024)}, f32[]{:T(128)}, f32[]{:T(128)}) all-reduce(f32[1024]{0:T(1024)S(1)} %get-tuple-element.384, f32[1024]{0:T(1024)S(1)} %copy-done.32, f32[]{:T(128)} %fusion.47, f32[]{:T(128)} %get-tuple-element.459), channel_id=1, replica_groups=mesh['dp'=4,'blk'=8] {'dp','blk'}, use_global_device_ids=true, to_apply=%region_30.31 | all-reduce | flops 2050 | bytes 16400 | tf_op jit(solution)/shard_map/psum | solution.py:327
  1602.9 62.8 %reduce-scatter.48.cloned.1.call-done = bf16[128,256]{1,0:T(8,128)(2,1)} async-done(((bf16[1024,256]{1,0:T(8,128)(2,1)}), bf16[128,256]{1,0:T(8,128)(2,1)}) %reduce-scatter.48.cloned.1.call-update) | async-done | bytes 65552
  1667.3 62.6 %reduce-scatter.46.cloned.1.call-done = bf16[128,256]{1,0:T(8,128)(2,1)} async-done(((bf16[1024,256]{1,0:T(8,128)(2,1)}), bf16[128,256]{1,0:T(8,128)(2,1)}) %reduce-scatter.46.cloned.1.call-update) | async-done | bytes 65552
  (309 shorter events, 500.7 us)
Async XLA Ops:
  7.2 134.5 %all-gather.5.cloned.1.call-start = ((), (), s32[]{:S(2)}) async-start(), calls=%async_computation.16 | async-start | bytes 9437184 | tf_op jit(solution)/shard_map/all_gather | solution.py:147
  9.1 18.2 %copy-start.28 = (f32[256,2]{0,1:T(2,128)}, f32[256,2]{0,1:T(2,128)S(1)}, u32[]{:S(2)}) copy-start(f32[256,2]{0,1:T(2,128)S(1)} %add_rsqrt_fusion.1) | copy-start | bytes 6148
  13.9 253.7 %all-gather.3.cloned.1.call-start = ((), (), s32[]{:S(2)}) async-start(), calls=%async_computation.15 | async-start | bytes 9437184 | tf_op jit(solution)/shard_map/all_gather | solution.py:146
  31.8 928.8 %reduce-scatter.30.cloned.1.call-start = ((), (), s32[]{:S(2)}) async-start(), calls=%async_computation.17 | async-start | bytes 18874368 | tf_op jit(solution)/shard_map/reduce_scatter | solution.py:259
  427.8 29.2 %copy-start.3 = (f32[256,2,1024]{2,0,1:T(8,128)}, f32[256,2,1024]{2,0,1:T(8,128)S(1)}, u32[]{:S(2)}) copy-start(f32[256,2,1024]{2,0,1:T(8,128)S(1)} %get-tuple-element.470) | copy-start | bytes 6291460
  428.1 18.9 %slice-start = ((s8[5767168]{0:T(1024)(128)(4,1)}), s8[4194304]{0:T(1024)(128)(4,1)S(1)}, s32[]{:S(2)}) async-start(s8[5767168]{0:T(1024)(128)(4,1)} %bitcast.283), calls=%async_computation.32 | async-start | bytes 8388608
  436.6 10.4 slice-start.1
  680.4 313.9 %reduce-scatter.38.cloned.1.call-start = ((), (), s32[]{:S(2)}) async-start(), calls=%async_computation.21 | async-start | bytes 2621440 | tf_op jit(solution)/shard_map/reduce_scatter | solution.py:291
  685.8 365.8 %reduce-scatter.40.cloned.1.call-start = ((), (), s32[]{:S(2)}) async-start(), calls=%async_computation.22 | async-start | bytes 7208960 | tf_op jit(solution)/shard_map/reduce_scatter | solution.py:294
  693.9 415.1 %reduce-scatter.42.cloned.1.call-start = ((), (), s32[]{:S(2)}) async-start(), calls=%async_computation.23 | async-start | bytes 7208960 | tf_op jit(solution)/shard_map/reduce_scatter | solution.py:297
  700.8 465.7 %reduce-scatter.44.cloned.1.call-start = ((), (), s32[]{:S(2)}) async-start(), calls=%async_computation.24 | async-start | bytes 7208960 | tf_op jit(solution)/shard_map/reduce_scatter | solution.py:300
  709.0 255.9 %copy-start.7 = (bf16[256,2,1024]{2,1,0:T(2,128)(2,1)S(1)}, bf16[256,2,1024]{2,1,0:T(2,128)(2,1)}, u32[]{:S(2)}) copy-start(bf16[256,2,1024]{2,1,0:T(2,128)(2,1)} %param.17) | copy-start | bytes 3145732
  709.0 255.9 %copy-start.27 = (f32[1024]{0:T(1024)S(1)}, f32[1024]{0:T(1024)}, u32[]{:S(2)}) copy-start(f32[1024]{0:T(1024)} %param.27) | copy-start | bytes 12292
  709.0 255.9 %copy-start.29 = (f32[256,2]{0,1:T(2,128)S(1)}, f32[256,2]{0,1:T(2,128)}, u32[]{:S(2)}) copy-start(f32[256,2]{0,1:T(2,128)} %copy-done.28) | copy-start | bytes 6148
  709.0 491.7 %reduce-scatter.36.cloned.1.call-start = ((), (), s32[]{:S(2)}) async-start(), calls=%async_computation.20 | async-start | bytes 2621440 | tf_op jit(solution)/shard_map/reduce_scatter | solution.py:288
  967.8 298.1 %reduce-scatter.52.cloned.1.call-start = ((), (), s32[]{:S(2)}) async-start(), calls=%async_computation.28 | async-start | bytes 589824
  996.3 337.2 %reduce-scatter.54.cloned.1.call-start = ((), (), s32[]{:S(2)}) async-start(), calls=%async_computation.29 | async-start | bytes 1622016
  1054.2 347.0 %reduce-scatter.56.cloned.1.call-start = ((), (), s32[]{:S(2)}) async-start(), calls=%async_computation.30 | async-start | bytes 1622016
  1111.6 357.0 %reduce-scatter.58.cloned.1.call-start = ((), (), s32[]{:S(2)}) async-start(), calls=%async_computation.31 | async-start | bytes 1769472
  1169.1 333.0 %reduce-scatter.34.cloned.1.call-start = ((), (), s32[]{:S(2)}) async-start(), calls=%async_computation.19 | async-start | bytes 2621440 | tf_op jit(solution)/shard_map/reduce_scatter | solution.py:285
  1183.1 353.0 %reduce-scatter.32.cloned.1.call-start = ((), (), s32[]{:S(2)}) async-start(), calls=%async_computation.18 | async-start | bytes 2621440 | tf_op jit(solution)/shard_map/reduce_scatter | solution.py:282
  1187.4 413.8 %reduce-scatter.50.cloned.1.call-start = ((), (), s32[]{:S(2)}) async-start(), calls=%async_computation.27 | async-start | bytes 589824
  1202.7 463.0 %reduce-scatter.48.cloned.1.call-start = ((), (), s32[]{:S(2)}) async-start(), calls=%async_computation.26 | async-start | bytes 589824
  1504.1 225.8 %reduce-scatter.46.cloned.1.call-start = ((), (), s32[]{:S(2)}) async-start(), calls=%async_computation.25 | async-start | bytes 589824
  (37 other events, 148.3 us)
Sparse Core Ops, SparseCore 0:
  14.1 127.5 all-gather.4
  144.5 123.0 all-gather.2
  680.5 280.1 reduce-scatter.29
  963.8 30.4 reduce-scatter.37
  996.7 54.8 reduce-scatter.39
  1054.1 54.8 reduce-scatter.41
  1111.6 54.8 reduce-scatter.43
  1169.2 31.4 reduce-scatter.35
  1204.0 61.8 reduce-scatter.51
  1269.6 63.9 reduce-scatter.53
  1337.4 63.8 reduce-scatter.55
  1404.9 63.6 reduce-scatter.57
  1471.7 30.3 reduce-scatter.33
  1504.6 31.4 reduce-scatter.31
  1539.3 61.9 reduce-scatter.49
  1604.8 60.8 reduce-scatter.47
  1668.9 60.9 reduce-scatter.45
where the time goes:
time: 1750 us; the launch traced here: 1740 us
  waiting for transfers between devices  1110 us (63%)
  matrix products  317 us (18%)
  local copies, waits for them, and re-layouts  150 us (9%)
  other arithmetic  89.3 us (5%)
  blocking collectives  39.7 us (2%)
  between operations  18.2 us (1%)
    unnamed x24, waiting for transfers between devices  385 us
    reduce_scatter x1, waiting for transfers between devices, body(): lax.psum_scatter(terms.astype(jnp.bfloat16), 'blk', scatter_dimension=0,...  252 us
    all_gather x1, waiting for transfers between devices, body(): key_piece = lax.all_gather(keys_rot, 'blk', axis=0, tiled=True)  114 us
    all_gather x1, waiting for transfers between devices, body(): value_piece = lax.all_gather(mixed_low, 'blk', axis=0, tiled=True)  99.5 us
    unnamed x95, local copies, waits for them, and re-layouts  72 us
    reduce_scatter x1, waiting for transfers between devices, body(): lax.psum_scatter(weight_grads[4].astype(jnp.bfloat16), 'dp', scatter_dime...  55.2 us
    reduce_scatter x1, waiting for transfers between devices, body(): lax.psum_scatter(weight_grads[6].astype(jnp.bfloat16), 'dp', scatter_dime...  54.8 us
    reduce_scatter x1, waiting for transfers between devices, body(): lax.psum_scatter(weight_grads[5].astype(jnp.bfloat16), 'dp', scatter_dime...  54.8 us
  transfers between devices with their start and end apart: 17, of which 17 were waited for; matrix products, arithmetic and copies ran while one was open for 8% of the time, Pallas kernels for 0%

commit v1 on v0

--- a/solution.py
+++ b/solution.py
@@ -143,8 +143,11 @@
         jnp.zeros((seq_count, HEADS, local_len, HEAD_DIM), jnp.float32),
     )
     running = start_state
-    key_piece = lax.all_gather(keys_rot, "blk", axis=0, tiled=True)
-    value_piece = lax.all_gather(mixed_low, "blk", axis=0, tiled=True)
+    key_piece, value_piece = jnp.split(
+        lax.all_gather(jnp.concatenate([keys_rot, mixed_low], axis=1), "blk", axis=0, tiled=True),
+        [keys_rot.shape[1]],
+        axis=1,
+    )
     n_keys = key_piece.shape[0]
     step_rows = min(512, n_keys)
     n_steps = n_keys // step_rows

time: 1750 us -> 1850 us (1.057)
  local copies, waits for them, and re-layouts: 150 us -> 206 us
  matrix products: 317 us -> 340 us
    dynamic_slice x16 -> x32, local copies, waits for them, and re-layouts: 35.2 us -> 105 us  [body(): lax.scan(inner_step, running, (key_piece.reshape(n_steps, step_rows, seq_...]
    unnamed x95 -> x89, local copies, waits for them, and re-layouts: 72 us -> 49.2 us
    all_gather x2 -> x3, waiting for transfers between devices: 214 us -> 221 us  [the longest x1 218 us: body(): lax.all_gather(jnp.concatenate([keys_rot, mixed_low], axis=1), 'blk', axi...]
    unnamed x24 -> x25, waiting for transfers between devices: 385 us -> 386 us
  transfers between devices with their start and end apart: 17 -> 18, of which waited for: 17 -> 17; matrix products, arithmetic and copies ran while one was open for 8% -> 19% of each run, Pallas kernels for 0% -> 0%
where the time goes in v1:
time: 1850 us; the launch traced here: 1840 us
  waiting for transfers between devices  1120 us (61%)
  matrix products  340 us (18%)
  local copies, waits for them, and re-layouts  206 us (11%)
  other arithmetic  96.8 us (5%)
  blocking collectives  39.7 us (2%)
  between operations  18.6 us (1%)
    unnamed x25, waiting for transfers between devices  386 us
    reduce_scatter x1, waiting for transfers between devices, body(): lax.psum_scatter(terms.astype(jnp.bfloat16), 'blk', scatter_dimension=0,...  252 us
    all_gather x1, waiting for transfers between devices, body(): lax.all_gather(jnp.concatenate([keys_rot, mixed_low], axis=1), 'blk', axi...  218 us
    dynamic_slice x32, local copies, waits for them, and re-layouts, body(): lax.scan(inner_step, running, (key_piece.reshape(n_steps, step_rows, seq_...  105 us
    reduce_scatter x1, waiting for transfers between devices, body(): lax.psum_scatter(weight_grads[4].astype(jnp.bfloat16), 'dp', scatter_dime...  55.2 us
    reduce_scatter x1, waiting for transfers between devices, body(): lax.psum_scatter(weight_grads[5].astype(jnp.bfloat16), 'dp', scatter_dime...  55 us
    reduce_scatter x1, waiting for transfers between devices, body(): lax.psum_scatter(weight_grads[6].astype(jnp.bfloat16), 'dp', scatter_dime...  54.8 us
    unnamed x89, local copies, waits for them, and re-layouts  49.2 us
  transfers between devices with their start and end apart: 18, of which 17 were waited for; matrix products, arithmetic and copies ran while one was open for 19% of the time, Pallas kernels for 0%

profile of v1, /device:TPU:0, one launch (start us, length us, event | category | flops | bytes accessed | tf_op | source)
XLA Modules:
  0.0 1835.4 jit_solution(2501318408022098649)
XLA Ops:
  55.0 217.7 %all-gather.4.cloned.1.call-done = bf16[2048,4,1024]{2,0,1:T(8,128)(2,1)} async-done(((bf16[256,4,1024]{2,0,1:T(8,128)(2,1)}), bf16[2048,4,1024]{2,0,1:T(8,128)(2,1)}) %all-gather.4.cloned.1.call-update) | async-done | bytes 16777232 | tf_op jit(solution)/shard_map/all_gather | solution.py:147
  272.7 12.6 fusion.101
  285.2 193.7 %while.28 = (s32[]{:T(128)}, f32[2,16,256]{2,1,0:T(8,128)S(1)}, f32[2,16,256]{2,1,0:T(8,128)S(1)}, f32[2,16,256,64]{2,3,1,0:T(8,128)}, s32[4]{0:T(128)S(1)}, /*i...) while((s32[]{:T(128)}, f32[2,16,256]{2,1,0:T(8,128)S(1)}, ...), condition=%wide.region_7.8_spmd.clone, body=%wide.region_4.0_spmd.clone.sunk | while | flops 1122149120 | bytes 78401752 | solution.py:159
  321.5 12.1 fusion.162
  370.0 12.0 fusion.162
  419.1 11.8 fusion.162
  467.1 11.7 fusion.162
  523.9 229.1 %while.29 = (s32[]{:T(128)}, f32[256,2,16,64]{0,3,2,1:T(8,128)}, bf16[4,512,2,2048]{1,3,2,0:T(8,128)(2,1)}, bf16[4,512,2,1024]{3,1,0,2:T(8,128)(2,1)}, s32[4]{0:...) while((s32[]{:T(128)}, f32[256,2,16,64]{0,3,2,1:T(8,128)}, ...), condition=%wide.region_12.13_spmd.clone, body=%wide.region_11.12_spmd.clone.sunk | while | flops 2739012352 | bytes 129093896 | solution.py:252
  752.9 21.7 %copy.153 = bf16[4,512,2,2048]{3,1,0,2:T(8,128)(2,1)} copy(bf16[4,512,2,2048]{1,3,2,0:T(8,128)(2,1)} %get-tuple-element.145) | data formatting | bytes 33554432 | tf_op jit(solution)/shard_map/convert_element_type | solution.py:263
  803.4 251.6 %reduce-scatter.30.cloned.1.call-done = bf16[256,2,2048]{2,0,1:T(8,128)(2,1)} async-done(((bf16[2048,2,2048]{2,0,1:T(8,128)(2,1)}), bf16[256,2,2048]{2,0,1:T(8,128)(2,1)}) %reduce-scatter.30.cloned.1.call-update) | async-done | bytes 2097168 | tf_op jit(solution)/shard_map/reduce_scatter | solution.py:262
  1062.1 26.5 %reduce-scatter.38.cloned.1.call-done = bf16[256,1024]{1,0:T(8,128)(2,1)} async-done(((bf16[1024,1024]{1,0:T(8,128)(2,1)}), bf16[256,1024]{1,0:T(8,128)(2,1)}) %reduce-scatter.38.cloned.1.call-update) | async-done | bytes 524304 | tf_op jit(solution)/shard_map/reduce_scatter | solution.py:294
  1090.7 55.2 %reduce-scatter.40.cloned.1.call-done = bf16[256,2816]{1,0:T(8,128)(2,1)} async-done(((bf16[1024,2816]{1,0:T(8,128)(2,1)}), bf16[256,2816]{1,0:T(8,128)(2,1)}) %reduce-scatter.40.cloned.1.call-update) | async-done | bytes 1441808 | tf_op jit(solution)/shard_map/reduce_scatter | solution.py:297
  1148.5 55.0 %reduce-scatter.42.cloned.1.call-done = bf16[256,2816]{1,0:T(8,128)(2,1)} async-done(((bf16[1024,2816]{1,0:T(8,128)(2,1)}), bf16[256,2816]{1,0:T(8,128)(2,1)}) %reduce-scatter.42.cloned.1.call-update) | async-done | bytes 1441808 | tf_op jit(solution)/shard_map/reduce_scatter | solution.py:300
  1206.1 54.8 %reduce-scatter.44.cloned.1.call-done = bf16[704,1024]{1,0:T(8,128)(2,1)} async-done(((bf16[2816,1024]{1,0:T(8,128)(2,1)}), bf16[704,1024]{1,0:T(8,128)(2,1)}) %reduce-scatter.44.cloned.1.call-update) | async-done | bytes 1441808 | tf_op jit(solution)/shard_map/reduce_scatter | solution.py:303
  1281.8 13.3 reduce-scatter.36.cloned.1.call-done
  1308.9 51.3 %reduce-scatter.52.cloned.1.call-done = bf16[128,256]{1,0:T(8,128)(2,1)} async-done(((bf16[1024,256]{1,0:T(8,128)(2,1)}), bf16[128,256]{1,0:T(8,128)(2,1)}) %reduce-scatter.52.cloned.1.call-update) | async-done | bytes 65552
  1361.9 66.0 %reduce-scatter.54.cloned.1.call-done = bf16[352,256]{1,0:T(8,128)(2,1)} async-done(((bf16[2816,256]{1,0:T(8,128)(2,1)}), bf16[352,256]{1,0:T(8,128)(2,1)}) %reduce-scatter.54.cloned.1.call-update) | async-done | bytes 180240
  1429.8 65.8 %reduce-scatter.56.cloned.1.call-done = bf16[352,256]{1,0:T(8,128)(2,1)} async-done(((bf16[2816,256]{1,0:T(8,128)(2,1)}), bf16[352,256]{1,0:T(8,128)(2,1)}) %reduce-scatter.56.cloned.1.call-update) | async-done | bytes 180240
  1497.6 65.7 %reduce-scatter.58.cloned.1.call-done = bf16[128,704]{1,0:T(8,128)(2,1)} async-done(((bf16[1024,704]{1,0:T(8,128)(2,1)}), bf16[128,704]{1,0:T(8,128)(2,1)}) %reduce-scatter.58.cloned.1.call-update) | async-done | bytes 180240
  1565.2 31.5 %reduce-scatter.34.cloned.1.call-done = bf16[256,1024]{1,0:T(8,128)(2,1)} async-done(((bf16[1024,1024]{1,0:T(8,128)(2,1)}), bf16[256,1024]{1,0:T(8,128)(2,1)}) %reduce-scatter.34.cloned.1.call-update) | async-done | bytes 524304 | tf_op jit(solution)/shard_map/reduce_scatter | solution.py:288
  1609.0 21.6 %reduce-scatter.32.cloned.1.call-done = bf16[256,1024]{1,0:T(8,128)(2,1)} async-done(((bf16[1024,1024]{1,0:T(8,128)(2,1)}), bf16[256,1024]{1,0:T(8,128)(2,1)}) %reduce-scatter.32.cloned.1.call-update) | async-done | bytes 524304 | tf_op jit(solution)/shard_map/reduce_scatter | solution.py:285
  1638.7 39.7 %all-reduce = (f32[1024]{0:T(1024)}, f32[1024]{0:T(1024)}, f32[]{:T(128)}, f32[]{:T(128)}) all-reduce(f32[1024]{0:T(1024)S(1)} %get-tuple-element.384, f32[1024]{0:T(1024)S(1)} %copy-done.29, f32[]{:T(128)} %fusion.47, f32[]{:T(128)} %get-tuple-element.461), channel_id=1, replica_groups=mesh['dp'=4,'blk'=8] {'dp','blk'}, use_global_device_ids=true, to_apply=%region_30.31 | all-reduce | flops 2050 | bytes 16400 | tf_op jit(solution)/shard_map/psum | solution.py:330
  1697.5 62.9 %reduce-scatter.48.cloned.1.call-done = bf16[128,256]{1,0:T(8,128)(2,1)} async-done(((bf16[1024,256]{1,0:T(8,128)(2,1)}), bf16[128,256]{1,0:T(8,128)(2,1)}) %reduce-scatter.48.cloned.1.call-update) | async-done | bytes 65552
  1762.0 62.5 %reduce-scatter.46.cloned.1.call-done = bf16[128,256]{1,0:T(8,128)(2,1)} async-done(((bf16[1024,256]{1,0:T(8,128)(2,1)}), bf16[128,256]{1,0:T(8,128)(2,1)}) %reduce-scatter.46.cloned.1.call-update) | async-done | bytes 65552
  (316 shorter events, 577.3 us)
Async XLA Ops:
  7.2 27.5 %copy-start = (bf16[1024,1024]{1,0:T(8,128)(2,1)S(1)}, bf16[1024,1024]{1,0:T(8,128)(2,1)}, u32[]{:S(2)}) copy-start(bf16[1024,1024]{1,0:T(8,128)(2,1)} %param.22) | copy-start | bytes 6291460
  7.2 265.5 %all-gather.4.cloned.1.call-start = ((), (), s32[]{:S(2)}) async-start(), calls=%async_computation.15 | async-start | bytes 18874368 | tf_op jit(solution)/shard_map/all_gather | solution.py:147
  9.8 24.9 %copy-start.26 = (f32[256,2]{0,1:T(2,128)}, f32[256,2]{0,1:T(2,128)S(1)}, u32[]{:S(2)}) copy-start(f32[256,2]{0,1:T(2,128)S(1)} %add_rsqrt_fusion.1) | copy-start | bytes 6148
  42.2 478.7 %all-gather.8.cloned.1.call-start = ((), (), s32[]{:S(2)}) async-start(), calls=%async_computation.17 | async-start | bytes 9437184 | tf_op jit(solution)/shard_map/all_gather | solution.py:204
  43.0 480.9 %all-gather.6.cloned.1.call-start = ((), (), s32[]{:S(2)}) async-start(), calls=%async_computation.16 | async-start | bytes 9437184 | tf_op jit(solution)/shard_map/all_gather | solution.py:203
  43.7 1011.2 %reduce-scatter.30.cloned.1.call-start = ((), (), s32[]{:S(2)}) async-start(), calls=%async_computation.18 | async-start | bytes 18874368 | tf_op jit(solution)/shard_map/reduce_scatter | solution.py:262
  482.9 29.1 %copy-start.2 = (f32[256,2,1024]{2,0,1:T(8,128)}, f32[256,2,1024]{2,0,1:T(8,128)S(1)}, u32[]{:S(2)}) copy-start(f32[256,2,1024]{2,0,1:T(8,128)S(1)} %get-tuple-element.472) | copy-start | bytes 6291460
  774.7 313.9 %reduce-scatter.38.cloned.1.call-start = ((), (), s32[]{:S(2)}) async-start(), calls=%async_computation.22 | async-start | bytes 2621440 | tf_op jit(solution)/shard_map/reduce_scatter | solution.py:294
  780.1 365.8 %reduce-scatter.40.cloned.1.call-start = ((), (), s32[]{:S(2)}) async-start(), calls=%async_computation.23 | async-start | bytes 7208960 | tf_op jit(solution)/shard_map/reduce_scatter | solution.py:297
  788.2 415.3 %reduce-scatter.42.cloned.1.call-start = ((), (), s32[]{:S(2)}) async-start(), calls=%async_computation.24 | async-start | bytes 7208960 | tf_op jit(solution)/shard_map/reduce_scatter | solution.py:300
  795.1 465.8 %reduce-scatter.44.cloned.1.call-start = ((), (), s32[]{:S(2)}) async-start(), calls=%async_computation.25 | async-start | bytes 7208960 | tf_op jit(solution)/shard_map/reduce_scatter | solution.py:303
  803.3 255.8 %copy-start.6 = (bf16[256,2,1024]{2,1,0:T(2,128)(2,1)S(1)}, bf16[256,2,1024]{2,1,0:T(2,128)(2,1)}, u32[]{:S(2)}) copy-start(bf16[256,2,1024]{2,1,0:T(2,128)(2,1)} %param.17) | copy-start | bytes 3145732
  803.3 255.8 %copy-start.25 = (f32[1024]{0:T(1024)S(1)}, f32[1024]{0:T(1024)}, u32[]{:S(2)}) copy-start(f32[1024]{0:T(1024)} %param.27) | copy-start | bytes 12292
  803.3 255.8 %copy-start.27 = (f32[256,2]{0,1:T(2,128)S(1)}, f32[256,2]{0,1:T(2,128)}, u32[]{:S(2)}) copy-start(f32[256,2]{0,1:T(2,128)} %copy-done.26) | copy-start | bytes 6148
  803.3 491.7 %reduce-scatter.36.cloned.1.call-start = ((), (), s32[]{:S(2)}) async-start(), calls=%async_computation.21 | async-start | bytes 2621440 | tf_op jit(solution)/shard_map/reduce_scatter | solution.py:291
  1062.1 298.2 %reduce-scatter.52.cloned.1.call-start = ((), (), s32[]{:S(2)}) async-start(), calls=%async_computation.29 | async-start | bytes 589824
  1090.7 337.2 %reduce-scatter.54.cloned.1.call-start = ((), (), s32[]{:S(2)}) async-start(), calls=%async_computation.30 | async-start | bytes 1622016
  1148.4 347.2 %reduce-scatter.56.cloned.1.call-start = ((), (), s32[]{:S(2)}) async-start(), calls=%async_computation.31 | async-start | bytes 1622016
  1206.0 357.3 %reduce-scatter.58.cloned.1.call-start = ((), (), s32[]{:S(2)}) async-start(), calls=%async_computation.32 | async-start | bytes 1769472
  1263.5 333.1 %reduce-scatter.34.cloned.1.call-start = ((), (), s32[]{:S(2)}) async-start(), calls=%async_computation.20 | async-start | bytes 2621440 | tf_op jit(solution)/shard_map/reduce_scatter | solution.py:288
  1277.6 353.0 %reduce-scatter.32.cloned.1.call-start = ((), (), s32[]{:S(2)}) async-start(), calls=%async_computation.19 | async-start | bytes 2621440 | tf_op jit(solution)/shard_map/reduce_scatter | solution.py:285
  1281.7 414.1 %reduce-scatter.50.cloned.1.call-start = ((), (), s32[]{:S(2)}) async-start(), calls=%async_computation.28 | async-start | bytes 589824
  1297.2 463.2 %reduce-scatter.48.cloned.1.call-start = ((), (), s32[]{:S(2)}) async-start(), calls=%async_computation.27 | async-start | bytes 589824
  1598.7 225.8 %reduce-scatter.46.cloned.1.call-start = ((), (), s32[]{:S(2)}) async-start(), calls=%async_computation.26 | async-start | bytes 589824
  (32 other events, 160.3 us)
Sparse Core Ops, SparseCore 0:
  42.3 230.2 all-gather.3
  275.4 123.0 all-gather.7
  400.7 123.0 all-gather.5
  774.8 280.0 reduce-scatter.29
  1058.0 30.4 reduce-scatter.37
  1091.0 54.8 reduce-scatter.39
  1148.6 54.8 reduce-scatter.41
  1206.0 54.8 reduce-scatter.43
  1263.6 31.4 reduce-scatter.35
  1298.3 61.9 reduce-scatter.51
  1364.0 63.8 reduce-scatter.53
  1431.5 64.0 reduce-scatter.55
  1499.5 63.8 reduce-scatter.57
  1566.3 30.3 reduce-scatter.33
  1599.2 31.3 reduce-scatter.31
  1633.8 61.9 reduce-scatter.49
  1699.4 60.9 reduce-scatter.47
  1763.6 60.8 reduce-scatter.45
